TPU v7x, 512 devices: a whole 4x4x16 slice. The times are simulated.
512 devices in a mesh: dp: 32 (over z, core), seq: 16 (over y, x).
Axes of the slice: x: 4, y: 4, z: 16, core: 2. Of those that a mesh axis runs over, the one named last changes fastest.
Arguments:
- q_pre: bfloat16 [32, 2048, 16, 128], P('dp', 'seq'), may hold values from -6 to 6
- k_pre: bfloat16 [32, 2048, 8, 128], P('dp', 'seq'), may hold values from -6 to 6
- values: bfloat16 [32, 2048, 8, 128], P('dp', 'seq'), may hold values from -6 to 6
- grad_out: bfloat16 [32, 2048, 16, 128], P('dp', 'seq'), may hold values from -6 to 6
- segment_ids: int32 [32, 2048], P('dp', 'seq'), may hold values from 0 to 7, never falling along the last dimension, each value on 1 to 1024 neighbouring positions
- q_gain: float32 [128], replicated, may hold values from 0.1 to 1.9
- k_gain: float32 [128], replicated, may hold values from 0.1 to 1.9
Outputs:
- grad_q: bfloat16 [32, 2048, 16, 128], P('dp', 'seq')
- grad_k: bfloat16 [32, 2048, 8, 128], P('dp', 'seq')
- grad_v: bfloat16 [32, 2048, 8, 128], P('dp', 'seq')
- grad_q_gain: float32 [128], replicated
- grad_k_gain: float32 [128], replicated
Inputs may be any that keep to these rules, and one draw needn't show every extreme that they name: `segment_ids`: along a span the ids never fall, and each id from 0 to 7 names one run of consecutive tokens.
All inputs are finite; a program needn't handle non-finite values.
Results may differ from a plain program's by a relative error of at most 0.017.
Values may be sent and summed in bfloat16 or wider, within the bound.
A program may use at most 64 MiB of HBM per device.

v0:
```python
import jax
import jax.numpy as jnp
from jax import lax
from jax.sharding import PartitionSpec as P

PRESCALE = 168
DOCS = 8
norm_epsilon = 1e-06
rope_base = 1000000.0
rope_factor = 8.0


def document_positions(segments, docs):
    labels = jnp.arange(docs, dtype=jnp.int32)
    member = (segments[:, None] == labels[None, :]).astype(jnp.int32)
    counts = jnp.sum(member, axis=0)
    starts = jnp.cumsum(counts) - counts
    first = jnp.sum(member * starts[None, :], axis=1)
    return (jnp.arange(segments.shape[0], dtype=jnp.int32) - first, first)


def embed(rows, gain, positions):
    width = rows.shape[-1]
    half = width // 2
    scale = lax.rsqrt(jnp.mean(rows * rows, axis=-1, keepdims=True) + norm_epsilon)
    normed = rows * scale * gain
    freqs = rope_base ** (-(jnp.arange(half, dtype=jnp.float32) * 2.0 / width))
    angles = (positions.astype(jnp.float32) / rope_factor)[:, None] * freqs[None, :]
    cosine = jnp.cos(angles)[:, None, :]
    sine = jnp.sin(angles)[:, None, :]
    first_half = normed[..., :half]
    second_half = normed[..., half:]
    return jnp.concatenate(
        [first_half * cosine - second_half * sine, second_half * cosine + first_half * sine],
        axis=-1,
    )


def attend_blocks(queries, keys, vals, upstream, segments):
    total = queries.shape[0]
    group = queries.shape[1]
    width = queries.shape[2]
    block = min(512, total)
    count = total // block
    rows = block * group
    score_scale = float(PRESCALE) ** (-0.5)
    contract_last = (((1,), (1,)), ((), ()))
    contract_first = (((0,), (0,)), ((), ()))

    def query_block(query_index, carry):
        query_grads, key_grads, value_grads = carry
        start = query_index * block
        query_rows = lax.dynamic_slice_in_dim(queries, start, block, 0).reshape(rows, width)
        upstream_rows = lax.dynamic_slice_in_dim(upstream, start, block, 0).reshape(rows, width)
        query_segs = jnp.repeat(lax.dynamic_slice_in_dim(segments, start, block, 0), group)
        query_places = jnp.repeat(start + jnp.arange(block, dtype=jnp.int32), group)
        lower = 0

        def key_scores(key_index):
            key_start = key_index * block
            key_rows = lax.dynamic_slice_in_dim(keys, key_start, block, 0)
            value_rows = lax.dynamic_slice_in_dim(vals, key_start, block, 0)
            key_segs = lax.dynamic_slice_in_dim(segments, key_start, block, 0)
            key_places = key_start + jnp.arange(block, dtype=jnp.int32)
            scores = score_scale * lax.dot_general(
                query_rows, key_rows, contract_last, preferred_element_type=jnp.float32
            )
            visible = (query_segs[:, None] == key_segs[None, :]) & (
                query_places[:, None] >= key_places[None, :]
            )
            return (scores, visible, key_rows, value_rows, key_start)

        def forward_step(key_index, state):
            totals, numer = state
            scores, visible, key_rows, value_rows, key_start = key_scores(key_index)
            raw = jnp.where(visible, jnp.exp(scores), 0.0)
            numer = numer + jnp.dot(
                raw.astype(jnp.bfloat16), value_rows, preferred_element_type=jnp.float32
            )
            return (totals + jnp.sum(raw, axis=1), numer)

        totals, numer = lax.fori_loop(
            lower,
            query_index + 1,
            forward_step,
            (jnp.zeros((rows,), jnp.float32), jnp.zeros((rows, width), jnp.float32)),
        )
        outputs = numer / totals[:, None]
        delta = jnp.sum(upstream_rows.astype(jnp.float32) * outputs, axis=1)
        logsum = jnp.log(totals)

        def backward_step(key_index, state):
            query_part, key_acc, value_acc = state
            scores, visible, key_rows, value_rows, key_start = key_scores(key_index)
            probs = jnp.where(visible, jnp.exp(scores - logsum[:, None]), 0.0).astype(jnp.bfloat16)
            prob_grads = lax.dot_general(
                upstream_rows, value_rows, contract_last, preferred_element_type=jnp.float32
            )
            score_grads = (
                probs.astype(jnp.float32) * (prob_grads - delta[:, None]) * score_scale
            ).astype(jnp.bfloat16)
            query_part = query_part + jnp.dot(
                score_grads, key_rows, preferred_element_type=jnp.float32
            )
            key_part = lax.dot_general(
                score_grads, query_rows, contract_first, preferred_element_type=jnp.float32
            )
            value_part = lax.dot_general(
                probs, upstream_rows, contract_first, preferred_element_type=jnp.float32
            )
            key_acc = lax.dynamic_update_slice_in_dim(
                key_acc,
                lax.dynamic_slice_in_dim(key_acc, key_start, block, 0) + key_part,
                key_start,
                0,
            )
            value_acc = lax.dynamic_update_slice_in_dim(
                value_acc,
                lax.dynamic_slice_in_dim(value_acc, key_start, block, 0) + value_part,
                key_start,
                0,
            )
            return (query_part, key_acc, value_acc)

        query_part, key_grads, value_grads = lax.fori_loop(
            lower,
            query_index + 1,
            backward_step,
            (jnp.zeros((rows, width), jnp.float32), key_grads, value_grads),
        )
        query_grads = lax.dynamic_update_slice_in_dim(query_grads, query_part, start * group, 0)
        return (query_grads, key_grads, value_grads)

    initial = (
        jnp.zeros((total * group, width), jnp.float32),
        jnp.zeros((total, width), jnp.float32),
        jnp.zeros((total, width), jnp.float32),
    )
    query_grads, key_grads, value_grads = lax.fori_loop(0, count, query_block, initial)
    return (query_grads.reshape(total, group, width), key_grads, value_grads)


def body(q_pre, k_pre, values, grad_out, segment_ids, q_gain, k_gain):
    segments = lax.all_gather(segment_ids, "seq", axis=1, tiled=True)[0]
    positions, first = document_positions(segments, DOCS)
    local = q_pre.shape[1]
    heads = q_pre.shape[2]
    kv_heads = k_pre.shape[2]
    width = q_pre.shape[3]
    group = heads // kv_heads

    def embed_rows(rows, gain):
        return embed(rows, gain, positions)

    key_copies = jnp.repeat(k_pre[0], group, axis=1)
    value_copies = jnp.repeat(values[0], group, axis=1)
    query_here, upstream_here, key_here, value_here = (
        lax.all_to_all(q_pre[0], "seq", split_axis=1, concat_axis=0, tiled=True),
        lax.all_to_all(grad_out[0], "seq", split_axis=1, concat_axis=0, tiled=True),
        lax.all_to_all(key_copies, "seq", split_axis=1, concat_axis=0, tiled=True),
        lax.all_to_all(value_copies, "seq", split_axis=1, concat_axis=0, tiled=True),
    )
    query_rot, query_back = jax.vjp(embed_rows, query_here.astype(jnp.float32), q_gain)
    key_rot, key_back = jax.vjp(embed_rows, key_here.astype(jnp.float32), k_gain)
    query_hat = query_rot.astype(jnp.bfloat16)
    key_hat = key_rot.astype(jnp.bfloat16)
    query_list, key_list, value_list = ([], [], [])
    query_part, key_part, value_part = attend_blocks(
        query_hat, key_hat[:, 0], value_here[:, 0], upstream_here, segments
    )
    query_list.append(query_part)
    key_list.append(key_part)
    value_list.append(value_part)
    query_input, query_gain_part = query_back(query_list[0])
    key_input, key_gain_part = key_back(jnp.stack(key_list, axis=1))
    value_input = jnp.stack(value_list, axis=1)
    query_return, key_return, value_return = (
        lax.all_to_all(
            query_input.astype(jnp.bfloat16), "seq", split_axis=0, concat_axis=1, tiled=True
        ).astype(query_input.dtype),
        lax.all_to_all(
            key_input.astype(jnp.bfloat16), "seq", split_axis=0, concat_axis=1, tiled=True
        ).astype(key_input.dtype),
        lax.all_to_all(
            value_input.astype(jnp.bfloat16), "seq", split_axis=0, concat_axis=1, tiled=True
        ).astype(value_input.dtype),
    )
    grad_q = query_return.astype(jnp.bfloat16)
    grad_k = jnp.sum(key_return.reshape(local, kv_heads, group, width), axis=2).astype(jnp.bfloat16)
    grad_v = jnp.sum(value_return.reshape(local, kv_heads, group, width), axis=2).astype(
        jnp.bfloat16
    )
    gain_totals = lax.psum((query_gain_part, key_gain_part), ("dp", "seq"))
    return (grad_q[None], grad_k[None], grad_v[None], gain_totals[0], gain_totals[1])


def solution(mesh):
    return jax.shard_map(
        body,
        mesh=mesh,
        in_specs=(
            P("dp", "seq", None, None),
            P("dp", "seq", None, None),
            P("dp", "seq", None, None),
            P("dp", "seq", None, None),
            P("dp", "seq"),
            P(),
            P(),
        ),
        out_specs=(
            P("dp", "seq", None, None),
            P("dp", "seq", None, None),
            P("dp", "seq", None, None),
            P(),
            P(),
        ),
        check_vma=False,
    )
```

profile of v0, /device:TPU:1, one launch (start us, length us, event | category | flops | bytes accessed | tf_op | source)
XLA Modules:
  0.0 308.5 jit_solution(509402824562934716)
XLA Ops:
  0.6 2.0 copy.172
  2.6 7.7 %all-to-all-start = ((bf16[128,16,128]{2,0,1:T(8,128)(2,1)}), bf16[128,16,128]{2,0,1:T(8,128)(2,1)S(1)}, u32[]{:S(2)}, u32[]{:S(2)}) async-start(bf16[128,16,128]{2,0,1:T(8,128)(2,1)} %bitcast.130), calls=%async_computation | async-start | bytes 1048576 | tf_op jit(solution)/shard_map/all_to_all | solution.py:158
  10.4 17.6 %all_gather.3 = s32[1,2048]{1,0:T(1,128)S(1)} all-gather(s32[1,128]{1,0:T(1,128)S(1)} %copy-done.13), channel_id=1, replica_groups=mesh['dp'=32,'seq'=16] {'seq'}, dimensions={1}, use_global_device_ids=true | all-gather | bytes 8704 | tf_op jit(solution)/shard_map/all_gather | solution.py:144
  31.3 4.0 %all-to-all-start.1 = ((bf16[128,16,128]{0,2,1:T(8,128)(2,1)}), bf16[128,16,128]{0,2,1:T(8,128)(2,1)S(1)}, u32[]{:S(2)}, u32[]{:S(2)}) async-start(bf16[128,16,128]{0,2,1:T(8,128)(2,1)} %bitcast.12), calls=%async_computation.1 | async-start | bytes 1048576 | tf_op jit(solution)/shard_map/all_to_all | solution.py:160
  37.4 6.9 %all-to-all-done.1 = bf16[128,16,128]{0,2,1:T(8,128)(2,1)S(1)} async-done(((bf16[128,16,128]{0,2,1:T(8,128)(2,1)}), bf16[128,16,128]{0,2,1:T(8,128)(2,1)S(1)}, u32[]{:S(2)}, u32[]{:S(2)}) %all-to-all-start.1) | async-done | bytes 524320 | tf_op jit(solution)/shard_map/all_to_all | solution.py:160
  45.3 3.6 %all-to-all-start.2 = ((bf16[128,16,128]{2,0,1:T(8,128)(2,1)}), bf16[128,16,128]{2,0,1:T(8,128)(2,1)S(1)}, u32[]{:S(2)}, u32[]{:S(2)}) async-start(bf16[128,16,128]{2,0,1:T(8,128)(2,1)} %bitcast.20), calls=%async_computation.2 | async-start | bytes 1048576 | tf_op jit(solution)/shard_map/all_to_all | solution.py:161
  50.8 7.0 %all-to-all-done.2 = bf16[128,16,128]{2,0,1:T(8,128)(2,1)S(1)} async-done(((bf16[128,16,128]{2,0,1:T(8,128)(2,1)}), bf16[128,16,128]{2,0,1:T(8,128)(2,1)S(1)}, u32[]{:S(2)}, u32[]{:S(2)}) %all-to-all-start.2) | async-done | bytes 524320 | tf_op jit(solution)/shard_map/all_to_all | solution.py:161
  57.8 4.2 %all-to-all-start.3 = ((bf16[128,16,128]{2,0,1:T(8,128)(2,1)}), bf16[128,16,128]{2,0,1:T(8,128)(2,1)}, u32[]{:S(2)}, u32[]{:S(2)}) async-start(bf16[128,16,128]{2,0,1:T(8,128)(2,1)} %bitcast.129), calls=%async_computation.3 | async-start | bytes 1048576 | tf_op jit(solution)/shard_map/all_to_all | solution.py:159
  62.1 3.1 fusion.63
  66.2 4.8 %all-to-all-done.3 = bf16[128,16,128]{2,0,1:T(8,128)(2,1)} async-done(((bf16[128,16,128]{2,0,1:T(8,128)(2,1)}), bf16[128,16,128]{2,0,1:T(8,128)(2,1)}, u32[]{:S(2)}, u32[]{:S(2)}) %all-to-all-start.3) | async-done | bytes 524320 | tf_op jit(solution)/shard_map/all_to_all | solution.py:159
  72.3 69.1 %while.79 = (s32[]{:T(128)}, f32[2048,128]{0,1:T(8,128)}, f32[2048,128]{1,0:T(8,128)S(1)}, f32[2048,128]{1,0:T(8,128)S(1)}, bf16[2048,1,128]{0,2,1:T(8,128)(2,1)...) while((s32[]{:T(128)}, f32[2048,128]{0,1:T(8,128)}, ...), condition=%wide.region_12.13_spmd, body=%wide.region_5.12_spmd.sunk | while | flops 475268608 | bytes 14478353 | solution.py:139
  73.2 1.9 while.80
  73.3 1.4 fusion.101
  76.3 3.7 %while.81 = (s32[]{:T(128)}, f32[512,128]{1,0:T(8,128)S(1)}, f32[2048,128]{1,0:T(8,128)S(1)}, f32[2048,128]{1,0:T(8,128)S(1)}, s32[]{:T(128)}, /*index=5*/s32[51...) while((s32[]{:T(128)}, f32[512,128]{1,0:T(8,128)S(1)}, ...), condition=%wide.region_11.11_spmd.clone, body=%wide.region_10.10_spmd.clone.sunk | while | flops 338887680 | bytes 5656819 | solution.py:125
  76.4 1.4 fusion.112
  82.1 3.7 %while.80 = (s32[]{:T(128)}, f32[512]{0:T(512)S(1)}, f32[512,128]{1,0:T(8,128)S(1)}, s32[]{:T(128)}, s32[512]{0:T(512)S(1)}, /*index=5*/s32[2048]{0:T(1024)S(1)}...) while((s32[]{:T(128)}, f32[512]{0:T(512)S(1)}, ...), condition=%wide.region_8.8_spmd.clone, body=%wide.region_6.7_spmd.clone.sunk | while | flops 136119296 | bytes 1990855 | solution.py:82
  82.2 1.4 fusion.101
  84.1 1.4 fusion.101
  87.0 7.4 %while.81 = (s32[]{:T(128)}, f32[512,128]{1,0:T(8,128)S(1)}, f32[2048,128]{1,0:T(8,128)S(1)}, f32[2048,128]{1,0:T(8,128)S(1)}, s32[]{:T(128)}, /*index=5*/s32[51...) while((s32[]{:T(128)}, f32[512,128]{1,0:T(8,128)S(1)}, ...), condition=%wide.region_11.11_spmd.clone, body=%wide.region_10.10_spmd.clone.sunk | while | flops 338887680 | bytes 5656819 | solution.py:125
  87.1 1.4 fusion.112
  89.5 1.3 convolution_add_fusion.7
  90.9 1.4 fusion.112
  96.6 5.6 %while.80 = (s32[]{:T(128)}, f32[512]{0:T(512)S(1)}, f32[512,128]{1,0:T(8,128)S(1)}, s32[]{:T(128)}, s32[512]{0:T(512)S(1)}, /*index=5*/s32[2048]{0:T(1024)S(1)}...) while((s32[]{:T(128)}, f32[512]{0:T(512)S(1)}, ...), condition=%wide.region_8.8_spmd.clone, body=%wide.region_6.7_spmd.clone.sunk | while | flops 136119296 | bytes 1990855 | solution.py:82
  96.7 1.4 fusion.101
  98.6 1.4 fusion.101
  100.4 1.4 fusion.101
  103.4 11.1 %while.81 = (s32[]{:T(128)}, f32[512,128]{1,0:T(8,128)S(1)}, f32[2048,128]{1,0:T(8,128)S(1)}, f32[2048,128]{1,0:T(8,128)S(1)}, s32[]{:T(128)}, /*index=5*/s32[51...) while((s32[]{:T(128)}, f32[512,128]{1,0:T(8,128)S(1)}, ...), condition=%wide.region_11.11_spmd.clone, body=%wide.region_10.10_spmd.clone.sunk | while | flops 338887680 | bytes 5656819 | solution.py:125
  103.5 1.4 fusion.112
  107.2 1.4 fusion.112
  110.9 1.4 fusion.112
  116.6 7.5 %while.80 = (s32[]{:T(128)}, f32[512]{0:T(512)S(1)}, f32[512,128]{1,0:T(8,128)S(1)}, s32[]{:T(128)}, s32[512]{0:T(512)S(1)}, /*index=5*/s32[2048]{0:T(1024)S(1)}...) while((s32[]{:T(128)}, f32[512]{0:T(512)S(1)}, ...), condition=%wide.region_8.8_spmd.clone, body=%wide.region_6.7_spmd.clone.sunk | while | flops 136119296 | bytes 1990855 | solution.py:82
  116.7 1.4 fusion.101
  118.6 1.4 fusion.101
  120.5 1.4 fusion.101
  122.3 1.4 fusion.101
  125.3 14.8 %while.81 = (s32[]{:T(128)}, f32[512,128]{1,0:T(8,128)S(1)}, f32[2048,128]{1,0:T(8,128)S(1)}, f32[2048,128]{1,0:T(8,128)S(1)}, s32[]{:T(128)}, /*index=5*/s32[51...) while((s32[]{:T(128)}, f32[512,128]{1,0:T(8,128)S(1)}, ...), condition=%wide.region_11.11_spmd.clone, body=%wide.region_10.10_spmd.clone.sunk | while | flops 338887680 | bytes 5656819 | solution.py:125
  125.4 1.4 fusion.112
  129.1 1.4 fusion.112
  132.8 1.4 fusion.112
  136.5 1.4 fusion.112
  141.4 1.3 copy.139
  142.7 4.1 %fusion.60 = (f32[2048,1,64]{0,2,1:T(8,128)S(1)}, f32[2048,1,64]{0,2,1:T(8,128)S(1)}, f32[2048,1,64]{0,2,1:T(8,128)S(1)}, f32[2048,1,64]{0,2,1:T(8,128)S(1)}) fusion(f32[2048,1,128]{0,2,1:T(8,128)} %bitcast.158, f32[64]{0:T(128)S(1)} %negate_power_fusion, f32[2048]{0:T(1024)S(1)} %convert_multiply_fusion.1, f32[2048,1,128]{0,2,1:T(8,128)} %bitcast.157), kind=kLoop, calls=%fused_computation.89 | loop fusion | flops 1966080 | bytes 4202752 | tf_op jit(solution)/shard_map/transpose(jvp())/add_any | solution.py:34
  151.6 3.6 %all-to-all-start.4 = ((bf16[16,2,8192]{2,1,0:T(2,128)(2,1)}), bf16[16,2,8192]{2,1,0:T(2,128)(2,1)S(1)}, u32[]{:S(2)}, u32[]{:S(2)}) async-start(bf16[16,2,8192]{2,1,0:T(2,128)(2,1)} %reshape.576), calls=%async_computation.4 | async-start | bytes 1048576 | tf_op jit(solution)/shard_map/all_to_all | solution.py:178
  157.4 6.8 %all-to-all-done.4 = bf16[16,2,8192]{2,1,0:T(2,128)(2,1)S(1)} async-done(((bf16[16,2,8192]{2,1,0:T(2,128)(2,1)}), bf16[16,2,8192]{2,1,0:T(2,128)(2,1)S(1)}, u32[]{:S(2)}, u32[]{:S(2)}) %all-to-all-start.4) | async-done | bytes 524320 | tf_op jit(solution)/shard_map/all_to_all | solution.py:178
  164.1 3.6 %all-to-all-start.5 = ((bf16[16,2,8192]{2,1,0:T(2,128)(2,1)}), bf16[16,2,8192]{2,1,0:T(2,128)(2,1)S(1)}, u32[]{:S(2)}, u32[]{:S(2)}) async-start(bf16[16,2,8192]{2,1,0:T(2,128)(2,1)} %reshape.578), calls=%async_computation.5 | async-start | bytes 1048576 | tf_op jit(solution)/shard_map/all_to_all | solution.py:181
  169.7 9.0 %all-to-all-done.5 = bf16[16,2,8192]{2,1,0:T(2,128)(2,1)S(1)} async-done(((bf16[16,2,8192]{2,1,0:T(2,128)(2,1)}), bf16[16,2,8192]{2,1,0:T(2,128)(2,1)S(1)}, u32[]{:S(2)}, u32[]{:S(2)}) %all-to-all-start.5) | async-done | bytes 524320 | tf_op jit(solution)/shard_map/all_to_all | solution.py:181
  178.7 3.6 %all-to-all-start.6 = ((bf16[16,2,8192]{2,1,0:T(2,128)(2,1)}), bf16[16,2,8192]{2,1,0:T(2,128)(2,1)S(1)}, u32[]{:S(2)}, u32[]{:S(2)}) async-start(bf16[16,2,8192]{2,1,0:T(2,128)(2,1)} %reshape.580), calls=%async_computation.6 | async-start | bytes 1048576 | tf_op jit(solution)/shard_map/all_to_all | solution.py:184
  182.3 121.2 %all-reduce.4 = (f32[128]{0:T(128)}, f32[128]{0:T(128)}) all-reduce(f32[128]{0:T(128)S(1)} %get-tuple-element.430, f32[128]{0:T(128)S(1)} %get-tuple-element.428), channel_id=1, replica_groups=mesh['dp'=32,'seq'=16] {'dp','seq'}, use_global_device_ids=true, to_apply=%region_18.19 | all-reduce | flops 256 | bytes 2048 | tf_op jit(solution)/shard_map/psum | solution.py:193
  (232 shorter events, 63.7 us)
Async XLA Ops:
  2.6 7.7 %copy-start.13 = (s32[1,128]{1,0:T(1,128)S(1)}, s32[1,128]{1,0:T(1,128)}, u32[]{:S(2)}) copy-start(s32[1,128]{1,0:T(1,128)} %param.17) | copy-start | bytes 1540
  2.6 25.7 %copy-start.9 = (bf16[1,128,8,128]{3,2,1,0:T(8,128)(2,1)S(1)}, bf16[1,128,8,128]{3,2,1,0:T(8,128)(2,1)}, u32[]{:S(2)}) copy-start(bf16[1,128,8,128]{3,2,1,0:T(8,128)(2,1)} %param.14) | copy-start | bytes 786436
  2.6 27.8 %all-to-all-start = ((bf16[128,16,128]{2,0,1:T(8,128)(2,1)}), bf16[128,16,128]{2,0,1:T(8,128)(2,1)S(1)}, u32[]{:S(2)}, u32[]{:S(2)}) async-start(bf16[128,16,128]{2,0,1:T(8,128)(2,1)} %bitcast.130), calls=%async_computation | async-start | bytes 1048576 | tf_op jit(solution)/shard_map/all_to_all | solution.py:158
  10.3 18.2 %copy-start.10 = (bf16[1,128,8,128]{3,2,1,0:T(8,128)(2,1)S(1)}, bf16[1,128,8,128]{3,2,1,0:T(8,128)(2,1)}, u32[]{:S(2)}) copy-start(bf16[1,128,8,128]{3,2,1,0:T(8,128)(2,1)} %param.15) | copy-start | bytes 786436
  28.3 1.0 copy-start.8
  31.3 13.0 %all-to-all-start.1 = ((bf16[128,16,128]{0,2,1:T(8,128)(2,1)}), bf16[128,16,128]{0,2,1:T(8,128)(2,1)S(1)}, u32[]{:S(2)}, u32[]{:S(2)}) async-start(bf16[128,16,128]{0,2,1:T(8,128)(2,1)} %bitcast.12), calls=%async_computation.1 | async-start | bytes 1048576 | tf_op jit(solution)/shard_map/all_to_all | solution.py:160
  35.8 0.7 copy-start.12
  36.5 1.0 copy-start
  44.3 4.7 %copy-start.2 = (bf16[128,16,128]{0,2,1:T(8,128)(2,1)}, bf16[128,16,128]{0,2,1:T(8,128)(2,1)S(1)}, u32[]{:S(2)}) copy-start(bf16[128,16,128]{0,2,1:T(8,128)(2,1)S(1)} %all-to-all-done.1) | copy-start | bytes 1572868
  45.3 12.5 %all-to-all-start.2 = ((bf16[128,16,128]{2,0,1:T(8,128)(2,1)}), bf16[128,16,128]{2,0,1:T(8,128)(2,1)S(1)}, u32[]{:S(2)}, u32[]{:S(2)}) async-start(bf16[128,16,128]{2,0,1:T(8,128)(2,1)} %bitcast.20), calls=%async_computation.2 | async-start | bytes 1048576 | tf_op jit(solution)/shard_map/all_to_all | solution.py:161
  49.0 0.7 copy-start.11
  50.8 11.2 %copy-start.4 = (f32[2048,1,128]{0,2,1:T(8,128)S(1)}, f32[2048,1,128]{0,2,1:T(8,128)}, u32[]{:S(2)}) copy-start(f32[2048,1,128]{0,2,1:T(8,128)} %fusion.33) | copy-start | bytes 3145732
  57.8 13.2 %all-to-all-start.3 = ((bf16[128,16,128]{2,0,1:T(8,128)(2,1)}), bf16[128,16,128]{2,0,1:T(8,128)(2,1)}, u32[]{:S(2)}, u32[]{:S(2)}) async-start(bf16[128,16,128]{2,0,1:T(8,128)(2,1)} %bitcast.129), calls=%async_computation.3 | async-start | bytes 1048576 | tf_op jit(solution)/shard_map/all_to_all | solution.py:159
  65.2 1.0 copy-start.7
  72.4 0.8 copy-start.5
  80.1 1.1 copy-start.6
  81.3 0.8 copy-start.5
  94.6 1.1 copy-start.6
  95.7 0.8 copy-start.5
  114.6 1.1 copy-start.6
  115.8 0.8 copy-start.5
  140.3 1.1 copy-start.6
  142.7 4.1 %copy-start.3 = (bf16[128,16,128]{0,2,1:T(8,128)(2,1)S(1)}, bf16[128,16,128]{0,2,1:T(8,128)(2,1)}, u32[]{:S(2)}) copy-start(bf16[128,16,128]{0,2,1:T(8,128)(2,1)} %copy-done.2) | copy-start | bytes 1572868
  146.8 1.2 copy-start.1
  151.6 12.5 %all-to-all-start.4 = ((bf16[16,2,8192]{2,1,0:T(2,128)(2,1)}), bf16[16,2,8192]{2,1,0:T(2,128)(2,1)S(1)}, u32[]{:S(2)}, u32[]{:S(2)}) async-start(bf16[16,2,8192]{2,1,0:T(2,128)(2,1)} %reshape.576), calls=%async_computation.4 | async-start | bytes 1048576 | tf_op jit(solution)/shard_map/all_to_all | solution.py:178
  164.1 14.6 %all-to-all-start.5 = ((bf16[16,2,8192]{2,1,0:T(2,128)(2,1)}), bf16[16,2,8192]{2,1,0:T(2,128)(2,1)S(1)}, u32[]{:S(2)}, u32[]{:S(2)}) async-start(bf16[16,2,8192]{2,1,0:T(2,128)(2,1)} %reshape.578), calls=%async_computation.5 | async-start | bytes 1048576 | tf_op jit(solution)/shard_map/all_to_all | solution.py:181
  178.7 128.1 %all-to-all-start.6 = ((bf16[16,2,8192]{2,1,0:T(2,128)(2,1)}), bf16[16,2,8192]{2,1,0:T(2,128)(2,1)S(1)}, u32[]{:S(2)}, u32[]{:S(2)}) async-start(bf16[16,2,8192]{2,1,0:T(2,128)(2,1)} %reshape.580), calls=%async_computation.6 | async-start | bytes 1048576 | tf_op jit(solution)/shard_map/all_to_all | solution.py:184
where the time goes:
time: 310 us; the launch traced here: 308 us
  blocking collectives  139 us (45%)
  matrix products  53.1 us (17%)
  waiting for transfers between devices  34.4 us (11%)
  local copies, waits for them, and re-layouts  30.6 us (10%)
  starting transfers between devices  30.2 us (10%)
  other arithmetic  19 us (6%)
    psum x1, blocking collectives, body(): gain_totals = lax.psum((query_gain_part, key_gain_part), ('dp', 'seq'))  121 us
    dot_general x20, matrix products, key_scores(): lax.dot_general(query_rows, key_rows, contract_last, preferred_element_ty...  27.3 us
    all_gather x1, blocking collectives, body(): segments = lax.all_gather(segment_ids, 'seq', axis=1, tiled=True)[0]  17.6 us
    unnamed x40, local copies, waits for them, and re-layouts  14.1 us
    dot_general x10, matrix products, backward_step(): jnp.dot(score_grads, key_rows, preferred_element_type=jnp.float32)  12.8 us
    all_to_all x1, waiting for transfers between devices, body(): lax.all_to_all(key_input.astype(jnp.bfloat16), 'seq', split_axis=0, conca...  8.96 us
    all_to_all x1, starting transfers between devices, body(): lax.all_to_all(q_pre[0], 'seq', split_axis=1, concat_axis=0, tiled=True)  7.72 us
    all_to_all x1, waiting for transfers between devices, body(): lax.all_to_all(value_copies, 'seq', split_axis=1, concat_axis=0, tiled=True)  6.98 us
  transfers between devices with their start and end apart: 7, of which 5 were waited for; matrix products, arithmetic and copies ran while one was open for 5% of the time, Pallas kernels for 0%

commit v1 on v0

--- a/solution.py
+++ b/solution.py
@@ -8,6 +8,19 @@
 norm_epsilon = 1e-06
 rope_base = 1000000.0
 rope_factor = 8.0
+
+
+def ring_gather(x, axis, dim):
+    ways = lax.axis_size(axis)
+    up = [(d, (d + 1) % ways) for d in range(ways)]
+    down = [(d, (d - 1) % ways) for d in range(ways)]
+    earlier, later = ([x], [x])
+    for _ in range(ways // 2):
+        earlier.append(lax.ppermute(earlier[-1], axis, up))
+    for _ in range((ways - 1) // 2):
+        later.append(lax.ppermute(later[-1], axis, down))
+    line = jnp.concatenate([*earlier[::-1], *later[1:]], axis=dim)
+    return jnp.roll(line, (lax.axis_index(axis) - ways // 2) * x.shape[dim], axis=dim)
 
 
 def document_positions(segments, docs):
@@ -141,7 +154,7 @@
 
 
 def body(q_pre, k_pre, values, grad_out, segment_ids, q_gain, k_gain):
-    segments = lax.all_gather(segment_ids, "seq", axis=1, tiled=True)[0]
+    segments = ring_gather(segment_ids, "seq", 1)[0]
     positions, first = document_positions(segments, DOCS)
     local = q_pre.shape[1]
     heads = q_pre.shape[2]

time: 310 us -> 366 us (1.18)
  starting transfers between devices: 30.2 us -> 95.4 us
  blocking collectives: 139 us -> 121 us
  waiting for transfers between devices: 34.4 us -> 42.2 us
    ppermute x0 -> x15, starting transfers between devices: none -> 64.2 us  [the longest x7 46.8 us: ring_gather(): later.append(lax.ppermute(later[-1], axis, down))]
    all_gather x1 -> x0, blocking collectives: 17.6 us -> none  [body(): segments = lax.all_gather(segment_ids, 'seq', axis=1, tiled=True)[0]]
    ppermute x0 -> x15, waiting for transfers between devices: none -> 4.8 us  [the longest x8 4.79 us: ring_gather(): earlier.append(lax.ppermute(earlier[-1], axis, up))]
    unnamed x40 -> x71, local copies, waits for them, and re-layouts: 14.1 us -> 14.2 us
  transfers between devices with their start and end apart: 7 -> 22, of which waited for: 5 -> 6; matrix products, arithmetic and copies ran while one was open for 5% -> 5% of each run, Pallas kernels for 0% -> 0%
where the time goes in v1:
time: 366 us; the launch traced here: 364 us
  blocking collectives  121 us (33%)
  starting transfers between devices  95.4 us (26%)
  matrix products  53.1 us (15%)
  waiting for transfers between devices  42.2 us (12%)
  local copies, waits for them, and re-layouts  30.7 us (8%)
  other arithmetic  19 us (5%)
    psum x1, blocking collectives, body(): gain_totals = lax.psum((query_gain_part, key_gain_part), ('dp', 'seq'))  121 us
    ppermute x7, starting transfers between devices, ring_gather(): later.append(lax.ppermute(later[-1], axis, down))  46.8 us
    dot_general x20, matrix products, key_scores(): lax.dot_general(query_rows, key_rows, contract_last, preferred_element_ty...  27.3 us
    ppermute x8, starting transfers between devices, ring_gather(): earlier.append(lax.ppermute(earlier[-1], axis, up))  17.4 us
    unnamed x71, local copies, waits for them, and re-layouts  14.2 us
    dot_general x10, matrix products, backward_step(): jnp.dot(score_grads, key_rows, preferred_element_type=jnp.float32)  12.8 us
    all_to_all x1, waiting for transfers between devices, body(): lax.all_to_all(value_copies, 'seq', split_axis=1, concat_axis=0, tiled=True)  10.4 us
  transfers between devices with their start and end apart: 22, of which 6 were waited for; matrix products, arithmetic and copies ran while one was open for 5% of the time, Pallas kernels for 0%

profile of v1, /device:TPU:1, one launch (start us, length us, event | category | flops | bytes accessed | tf_op | source)
XLA Modules:
  0.0 363.6 jit_solution(11804515122698345449)
XLA Ops:
  0.6 4.0 %collective-permute-start = (s32[1,128]{1,0:T(1,128)}, s32[1,128]{1,0:T(1,128)S(1)}, u32[]{:S(2)}, u32[]{:S(2)}) collective-permute-start(s32[1,128]{1,0:T(1,128)} %param.17), channel_id=1, source_target_pairs={{0,1},{1,2},{2,3},{3,4},{4,5},{5,6},{6,7},{7,8},{8,9},{9,10},{10,1... | collective-permute-start | bytes 1544 | tf_op jit(solution)/shard_map/ppermute | solution.py:19
  4.6 4.8 %collective-permute-done = s32[1,128]{1,0:T(1,128)S(1)} collective-permute-done((s32[1,128]{1,0:T(1,128)}, s32[1,128]{1,0:T(1,128)S(1)}, u32[]{:S(2)}, u32[]{:S(2)}) %collective-permute-start) | collective-permute-done | bytes 544 | tf_op jit(solution)/shard_map/ppermute | solution.py:19
  9.4 1.9 collective-permute-start.1
  11.3 6.7 %collective-permute-start.8 = (s32[1,128]{1,0:T(1,128)}, s32[1,128]{1,0:T(1,128)S(1)}, u32[]{:S(2)}, u32[]{:S(2)}) collective-permute-start(s32[1,128]{1,0:T(1,128)} %param.17), channel_id=1, source_target_pairs={{0,15},{1,0},{2,1},{3,2},{4,3},{5,4},{6,5},{7,6},{8,7},{9,8},{10,9... | collective-permute-start | bytes 1544 | tf_op jit(solution)/shard_map/ppermute | solution.py:21
  18.0 1.9 collective-permute-start.2
  19.9 2.0 copy.172
  21.9 6.3 %all-to-all-start = ((bf16[128,16,128]{2,0,1:T(8,128)(2,1)}), bf16[128,16,128]{2,0,1:T(8,128)(2,1)S(1)}, u32[]{:S(2)}, u32[]{:S(2)}) async-start(bf16[128,16,128]{2,0,1:T(8,128)(2,1)} %bitcast.130), calls=%async_computation | async-start | bytes 1048576 | tf_op jit(solution)/shard_map/all_to_all | solution.py:171
  28.2 6.6 %collective-permute-start.9 = (s32[1,128]{1,0:T(1,128)S(1)}, s32[1,128]{1,0:T(1,128)S(1)}, u32[]{:S(2)}, u32[]{:S(2)}) collective-permute-start(s32[1,128]{1,0:T(1,128)S(1)} %collective-permute-done.8), channel_id=1, source_target_pairs={{0,15},{1,0},{2,1},{3,2},{4,3},{5,4},{6,5},{7,6},{8,7},{9,8},{10,9... | collective-permute-start | bytes 1544 | tf_op jit(solution)/shard_map/ppermute | solution.py:21
  34.8 1.9 collective-permute-start.3
  36.8 6.7 %collective-permute-start.10 = (s32[1,128]{1,0:T(1,128)S(1)}, s32[1,128]{1,0:T(1,128)S(1)}, u32[]{:S(2)}, u32[]{:S(2)}) collective-permute-start(s32[1,128]{1,0:T(1,128)S(1)} %collective-permute-done.9), channel_id=1, source_target_pairs={{0,15},{1,0},{2,1},{3,2},{4,3},{5,4},{6,5},{7,6},{8,7},{9,8},{10,9... | collective-permute-start | bytes 1544 | tf_op jit(solution)/shard_map/ppermute | solution.py:21
  43.5 1.9 collective-permute-start.4
  45.4 6.8 %collective-permute-start.11 = (s32[1,128]{1,0:T(1,128)S(1)}, s32[1,128]{1,0:T(1,128)S(1)}, u32[]{:S(2)}, u32[]{:S(2)}) collective-permute-start(s32[1,128]{1,0:T(1,128)S(1)} %collective-permute-done.10), channel_id=1, source_target_pairs={{0,15},{1,0},{2,1},{3,2},{4,3},{5,4},{6,5},{7,6},{8,7},{9,8},{10,9... | collective-permute-start | bytes 1544 | tf_op jit(solution)/shard_map/ppermute | solution.py:21
  52.2 1.9 collective-permute-start.5
  54.2 6.7 %collective-permute-start.12 = (s32[1,128]{1,0:T(1,128)S(1)}, s32[1,128]{1,0:T(1,128)S(1)}, u32[]{:S(2)}, u32[]{:S(2)}) collective-permute-start(s32[1,128]{1,0:T(1,128)S(1)} %collective-permute-done.11), channel_id=1, source_target_pairs={{0,15},{1,0},{2,1},{3,2},{4,3},{5,4},{6,5},{7,6},{8,7},{9,8},{10,9... | collective-permute-start | bytes 1544 | tf_op jit(solution)/shard_map/ppermute | solution.py:21
  60.9 1.9 collective-permute-start.6
  63.1 6.7 %collective-permute-start.13 = (s32[1,128]{1,0:T(1,128)S(1)}, s32[1,128]{1,0:T(1,128)S(1)}, u32[]{:S(2)}, u32[]{:S(2)}) collective-permute-start(s32[1,128]{1,0:T(1,128)S(1)} %collective-permute-done.12), channel_id=1, source_target_pairs={{0,15},{1,0},{2,1},{3,2},{4,3},{5,4},{6,5},{7,6},{8,7},{9,8},{10,9... | collective-permute-start | bytes 1544 | tf_op jit(solution)/shard_map/ppermute | solution.py:21
  69.8 1.9 collective-permute-start.7
  72.7 6.7 %collective-permute-start.14 = (s32[1,128]{1,0:T(1,128)S(1)}, s32[1,128]{1,0:T(1,128)S(1)}, u32[]{:S(2)}, u32[]{:S(2)}) collective-permute-start(s32[1,128]{1,0:T(1,128)S(1)} %collective-permute-done.13), channel_id=1, source_target_pairs={{0,15},{1,0},{2,1},{3,2},{4,3},{5,4},{6,5},{7,6},{8,7},{9,8},{10,9... | collective-permute-start | bytes 1544 | tf_op jit(solution)/shard_map/ppermute | solution.py:21
  81.8 6.2 %all-to-all-start.1 = ((bf16[128,16,128]{0,2,1:T(8,128)(2,1)}), bf16[128,16,128]{0,2,1:T(8,128)(2,1)S(1)}, u32[]{:S(2)}, u32[]{:S(2)}) async-start(bf16[128,16,128]{0,2,1:T(8,128)(2,1)} %bitcast.12), calls=%async_computation.1 | async-start | bytes 1048576 | tf_op jit(solution)/shard_map/all_to_all | solution.py:173
  90.1 6.9 %all-to-all-done.1 = bf16[128,16,128]{0,2,1:T(8,128)(2,1)S(1)} async-done(((bf16[128,16,128]{0,2,1:T(8,128)(2,1)}), bf16[128,16,128]{0,2,1:T(8,128)(2,1)S(1)}, u32[]{:S(2)}, u32[]{:S(2)}) %all-to-all-start.1) | async-done | bytes 524320 | tf_op jit(solution)/shard_map/all_to_all | solution.py:173
  98.0 3.6 all-to-all-start.2
  103.5 10.4 %all-to-all-done.2 = bf16[128,16,128]{2,0,1:T(8,128)(2,1)S(1)} async-done(((bf16[128,16,128]{2,0,1:T(8,128)(2,1)}), bf16[128,16,128]{2,0,1:T(8,128)(2,1)S(1)}, u32[]{:S(2)}, u32[]{:S(2)}) %all-to-all-start.2) | async-done | bytes 524320 | tf_op jit(solution)/shard_map/all_to_all | solution.py:174
  113.9 4.2 %all-to-all-start.3 = ((bf16[128,16,128]{2,0,1:T(8,128)(2,1)}), bf16[128,16,128]{2,0,1:T(8,128)(2,1)}, u32[]{:S(2)}, u32[]{:S(2)}) async-start(bf16[128,16,128]{2,0,1:T(8,128)(2,1)} %bitcast.129), calls=%async_computation.3 | async-start | bytes 1048576 | tf_op jit(solution)/shard_map/all_to_all | solution.py:172
  118.1 3.1 fusion.63
  122.3 6.4 %all-to-all-done.3 = bf16[128,16,128]{2,0,1:T(8,128)(2,1)} async-done(((bf16[128,16,128]{2,0,1:T(8,128)(2,1)}), bf16[128,16,128]{2,0,1:T(8,128)(2,1)}, u32[]{:S(2)}, u32[]{:S(2)}) %all-to-all-start.3) | async-done | bytes 524320 | tf_op jit(solution)/shard_map/all_to_all | solution.py:172
  130.0 69.0 %while.79 = (s32[]{:T(128)}, f32[2048,128]{0,1:T(8,128)}, f32[2048,128]{1,0:T(8,128)S(1)}, f32[2048,128]{1,0:T(8,128)S(1)}, bf16[2048,1,128]{0,2,1:T(8,128)(2,1)...) while((s32[]{:T(128)}, f32[2048,128]{0,1:T(8,128)}, ...), condition=%wide.region_12.13_spmd, body=%wide.region_5.12_spmd.sunk | while | flops 475268608 | bytes 14478353 | solution.py:152
  130.9 1.9 while.80
  131.0 1.4 fusion.101
  133.9 3.7 %while.81 = (s32[]{:T(128)}, f32[512,128]{1,0:T(8,128)S(1)}, f32[2048,128]{1,0:T(8,128)S(1)}, f32[2048,128]{1,0:T(8,128)S(1)}, s32[]{:T(128)}, /*index=5*/s32[51...) while((s32[]{:T(128)}, f32[512,128]{1,0:T(8,128)S(1)}, ...), condition=%wide.region_11.11_spmd.clone, body=%wide.region_10.10_spmd.clone.sunk | while | flops 338887680 | bytes 5656819 | solution.py:138
  139.8 3.7 %while.80 = (s32[]{:T(128)}, f32[512]{0:T(512)S(1)}, f32[512,128]{1,0:T(8,128)S(1)}, s32[]{:T(128)}, s32[512]{0:T(512)S(1)}, /*index=5*/s32[2048]{0:T(1024)S(1)}...) while((s32[]{:T(128)}, f32[512]{0:T(512)S(1)}, ...), condition=%wide.region_8.8_spmd.clone, body=%wide.region_6.7_spmd.clone.sunk | while | flops 136119296 | bytes 1990855 | solution.py:95
  139.9 1.4 fusion.101
  144.7 7.4 %while.81 = (s32[]{:T(128)}, f32[512,128]{1,0:T(8,128)S(1)}, f32[2048,128]{1,0:T(8,128)S(1)}, f32[2048,128]{1,0:T(8,128)S(1)}, s32[]{:T(128)}, /*index=5*/s32[51...) while((s32[]{:T(128)}, f32[512,128]{1,0:T(8,128)S(1)}, ...), condition=%wide.region_11.11_spmd.clone, body=%wide.region_10.10_spmd.clone.sunk | while | flops 338887680 | bytes 5656819 | solution.py:138
  154.2 5.6 %while.80 = (s32[]{:T(128)}, f32[512]{0:T(512)S(1)}, f32[512,128]{1,0:T(8,128)S(1)}, s32[]{:T(128)}, s32[512]{0:T(512)S(1)}, /*index=5*/s32[2048]{0:T(1024)S(1)}...) while((s32[]{:T(128)}, f32[512]{0:T(512)S(1)}, ...), condition=%wide.region_8.8_spmd.clone, body=%wide.region_6.7_spmd.clone.sunk | while | flops 136119296 | bytes 1990855 | solution.py:95
  154.3 1.4 fusion.101
  156.2 1.4 fusion.101
  158.1 1.4 fusion.101
  161.0 11.1 %while.81 = (s32[]{:T(128)}, f32[512,128]{1,0:T(8,128)S(1)}, f32[2048,128]{1,0:T(8,128)S(1)}, f32[2048,128]{1,0:T(8,128)S(1)}, s32[]{:T(128)}, /*index=5*/s32[51...) while((s32[]{:T(128)}, f32[512,128]{1,0:T(8,128)S(1)}, ...), condition=%wide.region_11.11_spmd.clone, body=%wide.region_10.10_spmd.clone.sunk | while | flops 338887680 | bytes 5656819 | solution.py:138
  174.3 7.5 %while.80 = (s32[]{:T(128)}, f32[512]{0:T(512)S(1)}, f32[512,128]{1,0:T(8,128)S(1)}, s32[]{:T(128)}, s32[512]{0:T(512)S(1)}, /*index=5*/s32[2048]{0:T(1024)S(1)}...) while((s32[]{:T(128)}, f32[512]{0:T(512)S(1)}, ...), condition=%wide.region_8.8_spmd.clone, body=%wide.region_6.7_spmd.clone.sunk | while | flops 136119296 | bytes 1990855 | solution.py:95
  174.4 1.4 fusion.101
  176.2 1.4 fusion.101
  182.9 14.8 %while.81 = (s32[]{:T(128)}, f32[512,128]{1,0:T(8,128)S(1)}, f32[2048,128]{1,0:T(8,128)S(1)}, f32[2048,128]{1,0:T(8,128)S(1)}, s32[]{:T(128)}, /*index=5*/s32[51...) while((s32[]{:T(128)}, f32[512,128]{1,0:T(8,128)S(1)}, ...), condition=%wide.region_11.11_spmd.clone, body=%wide.region_10.10_spmd.clone.sunk | while | flops 338887680 | bytes 5656819 | solution.py:138
  200.4 4.1 %fusion.60 = (f32[2048,1,64]{0,2,1:T(8,128)S(1)}, f32[2048,1,64]{0,2,1:T(8,128)S(1)}, f32[2048,1,64]{0,2,1:T(8,128)S(1)}, f32[2048,1,64]{0,2,1:T(8,128)S(1)}) fusion(f32[2048,1,128]{0,2,1:T(8,128)} %bitcast.158, f32[64]{0:T(128)S(1)} %negate_power_fusion, f32[2048]{0:T(1024)S(1)} %convert_multiply_fusion.1, f32[2048,1,128]{0,2,1:T(8,128)} %bitcast.157), kind=kLoop, calls=%fused_computation.89 | loop fusion | flops 1966080 | bytes 4202752 | tf_op jit(solution)/shard_map/transpose(jvp())/add_any | solution.py:47
  209.2 3.6 all-to-all-start.4
  215.0 6.8 %all-to-all-done.4 = bf16[16,2,8192]{2,1,0:T(2,128)(2,1)S(1)} async-done(((bf16[16,2,8192]{2,1,0:T(2,128)(2,1)}), bf16[16,2,8192]{2,1,0:T(2,128)(2,1)S(1)}, u32[]{:S(2)}, u32[]{:S(2)}) %all-to-all-start.4) | async-done | bytes 524320 | tf_op jit(solution)/shard_map/all_to_all | solution.py:191
  221.8 3.8 %all-to-all-start.5 = ((bf16[16,2,8192]{2,1,0:T(2,128)(2,1)}), bf16[16,2,8192]{2,1,0:T(2,128)(2,1)S(1)}, u32[]{:S(2)}, u32[]{:S(2)}) async-start(bf16[16,2,8192]{2,1,0:T(2,128)(2,1)} %reshape.578), calls=%async_computation.5 | async-start | bytes 1048576 | tf_op jit(solution)/shard_map/all_to_all | solution.py:194
  227.5 6.9 %all-to-all-done.5 = bf16[16,2,8192]{2,1,0:T(2,128)(2,1)S(1)} async-done(((bf16[16,2,8192]{2,1,0:T(2,128)(2,1)}), bf16[16,2,8192]{2,1,0:T(2,128)(2,1)S(1)}, u32[]{:S(2)}, u32[]{:S(2)}) %all-to-all-start.5) | async-done | bytes 524320 | tf_op jit(solution)/shard_map/all_to_all | solution.py:194
  234.4 3.6 all-to-all-start.6
  238.0 120.6 %all-reduce.4 = (f32[128]{0:T(128)}, f32[128]{0:T(128)}) all-reduce(f32[128]{0:T(128)S(1)} %get-tuple-element.430, f32[128]{0:T(128)S(1)} %get-tuple-element.428), channel_id=1, replica_groups=mesh['dp'=32,'seq'=16] {'dp','seq'}, use_global_device_ids=true, to_apply=%region_18.19 | all-reduce | flops 256 | bytes 2048 | tf_op jit(solution)/shard_map/psum | solution.py:206
  (294 shorter events, 84.1 us)
Async XLA Ops:
  0.6 8.7 %collective-permute-start = (s32[1,128]{1,0:T(1,128)}, s32[1,128]{1,0:T(1,128)S(1)}, u32[]{:S(2)}, u32[]{:S(2)}) collective-permute-start(s32[1,128]{1,0:T(1,128)} %param.17), channel_id=1, source_target_pairs={{0,1},{1,2},{2,3},{3,4},{4,5},{5,6},{6,7},{7,8},{8,9},{9,10},{10,1... | collective-permute-start | bytes 1544 | tf_op jit(solution)/shard_map/ppermute | solution.py:19
  9.4 8.6 %collective-permute-start.1 = (s32[1,128]{1,0:T(1,128)S(1)}, s32[1,128]{1,0:T(1,128)S(1)}, u32[]{:S(2)}, u32[]{:S(2)}) collective-permute-start(s32[1,128]{1,0:T(1,128)S(1)} %collective-permute-done), channel_id=1, source_target_pairs={{0,1},{1,2},{2,3},{3,4},{4,5},{5,6},{6,7},{7,8},{8,9},{9,10},{10,1... | collective-permute-start | bytes 1544 | tf_op jit(solution)/shard_map/ppermute | solution.py:19
  11.3 16.9 %collective-permute-start.8 = (s32[1,128]{1,0:T(1,128)}, s32[1,128]{1,0:T(1,128)S(1)}, u32[]{:S(2)}, u32[]{:S(2)}) collective-permute-start(s32[1,128]{1,0:T(1,128)} %param.17), channel_id=1, source_target_pairs={{0,15},{1,0},{2,1},{3,2},{4,3},{5,4},{6,5},{7,6},{8,7},{9,8},{10,9... | collective-permute-start | bytes 1544 | tf_op jit(solution)/shard_map/ppermute | solution.py:21
  18.0 16.8 %collective-permute-start.2 = (s32[1,128]{1,0:T(1,128)S(1)}, s32[1,128]{1,0:T(1,128)S(1)}, u32[]{:S(2)}, u32[]{:S(2)}) collective-permute-start(s32[1,128]{1,0:T(1,128)S(1)} %collective-permute-done.1), channel_id=1, source_target_pairs={{0,1},{1,2},{2,3},{3,4},{4,5},{5,6},{6,7},{7,8},{8,9},{9,10},{10,1... | collective-permute-start | bytes 1544 | tf_op jit(solution)/shard_map/ppermute | solution.py:19
  21.9 41.0 %copy-start.9 = (bf16[1,128,8,128]{3,2,1,0:T(8,128)(2,1)S(1)}, bf16[1,128,8,128]{3,2,1,0:T(8,128)(2,1)}, u32[]{:S(2)}) copy-start(bf16[1,128,8,128]{3,2,1,0:T(8,128)(2,1)} %param.14) | copy-start | bytes 786436
  21.9 59.0 %all-to-all-start = ((bf16[128,16,128]{2,0,1:T(8,128)(2,1)}), bf16[128,16,128]{2,0,1:T(8,128)(2,1)S(1)}, u32[]{:S(2)}, u32[]{:S(2)}) async-start(bf16[128,16,128]{2,0,1:T(8,128)(2,1)} %bitcast.130), calls=%async_computation | async-start | bytes 1048576 | tf_op jit(solution)/shard_map/all_to_all | solution.py:171
  28.2 8.6 %collective-permute-start.9 = (s32[1,128]{1,0:T(1,128)S(1)}, s32[1,128]{1,0:T(1,128)S(1)}, u32[]{:S(2)}, u32[]{:S(2)}) collective-permute-start(s32[1,128]{1,0:T(1,128)S(1)} %collective-permute-done.8), channel_id=1, source_target_pairs={{0,15},{1,0},{2,1},{3,2},{4,3},{5,4},{6,5},{7,6},{8,7},{9,8},{10,9... | collective-permute-start | bytes 1544 | tf_op jit(solution)/shard_map/ppermute | solution.py:21
  34.8 8.7 %collective-permute-start.3 = (s32[1,128]{1,0:T(1,128)S(1)}, s32[1,128]{1,0:T(1,128)S(1)}, u32[]{:S(2)}, u32[]{:S(2)}) collective-permute-start(s32[1,128]{1,0:T(1,128)S(1)} %collective-permute-done.2), channel_id=1, source_target_pairs={{0,1},{1,2},{2,3},{3,4},{4,5},{5,6},{6,7},{7,8},{8,9},{9,10},{10,1... | collective-permute-start | bytes 1544 | tf_op jit(solution)/shard_map/ppermute | solution.py:19
  36.8 8.6 %collective-permute-start.10 = (s32[1,128]{1,0:T(1,128)S(1)}, s32[1,128]{1,0:T(1,128)S(1)}, u32[]{:S(2)}, u32[]{:S(2)}) collective-permute-start(s32[1,128]{1,0:T(1,128)S(1)} %collective-permute-done.9), channel_id=1, source_target_pairs={{0,15},{1,0},{2,1},{3,2},{4,3},{5,4},{6,5},{7,6},{8,7},{9,8},{10,9... | collective-permute-start | bytes 1544 | tf_op jit(solution)/shard_map/ppermute | solution.py:21
  43.5 8.8 %collective-permute-start.4 = (s32[1,128]{1,0:T(1,128)S(1)}, s32[1,128]{1,0:T(1,128)S(1)}, u32[]{:S(2)}, u32[]{:S(2)}) collective-permute-start(s32[1,128]{1,0:T(1,128)S(1)} %collective-permute-done.3), channel_id=1, source_target_pairs={{0,1},{1,2},{2,3},{3,4},{4,5},{5,6},{6,7},{7,8},{8,9},{9,10},{10,1... | collective-permute-start | bytes 1544 | tf_op jit(solution)/shard_map/ppermute | solution.py:19
  45.4 26.3 %copy-start.10 = (bf16[1,128,8,128]{3,2,1,0:T(8,128)(2,1)S(1)}, bf16[1,128,8,128]{3,2,1,0:T(8,128)(2,1)}, u32[]{:S(2)}) copy-start(bf16[1,128,8,128]{3,2,1,0:T(8,128)(2,1)} %param.15) | copy-start | bytes 786436
  45.4 8.8 %collective-permute-start.11 = (s32[1,128]{1,0:T(1,128)S(1)}, s32[1,128]{1,0:T(1,128)S(1)}, u32[]{:S(2)}, u32[]{:S(2)}) collective-permute-start(s32[1,128]{1,0:T(1,128)S(1)} %collective-permute-done.10), channel_id=1, source_target_pairs={{0,15},{1,0},{2,1},{3,2},{4,3},{5,4},{6,5},{7,6},{8,7},{9,8},{10,9... | collective-permute-start | bytes 1544 | tf_op jit(solution)/shard_map/ppermute | solution.py:21
  52.2 8.6 %collective-permute-start.5 = (s32[1,128]{1,0:T(1,128)S(1)}, s32[1,128]{1,0:T(1,128)S(1)}, u32[]{:S(2)}, u32[]{:S(2)}) collective-permute-start(s32[1,128]{1,0:T(1,128)S(1)} %collective-permute-done.4), channel_id=1, source_target_pairs={{0,1},{1,2},{2,3},{3,4},{4,5},{5,6},{6,7},{7,8},{8,9},{9,10},{10,1... | collective-permute-start | bytes 1544 | tf_op jit(solution)/shard_map/ppermute | solution.py:19
  54.2 8.9 %collective-permute-start.12 = (s32[1,128]{1,0:T(1,128)S(1)}, s32[1,128]{1,0:T(1,128)S(1)}, u32[]{:S(2)}, u32[]{:S(2)}) collective-permute-start(s32[1,128]{1,0:T(1,128)S(1)} %collective-permute-done.11), channel_id=1, source_target_pairs={{0,15},{1,0},{2,1},{3,2},{4,3},{5,4},{6,5},{7,6},{8,7},{9,8},{10,9... | collective-permute-start | bytes 1544 | tf_op jit(solution)/shard_map/ppermute | solution.py:21
  60.9 8.9 %collective-permute-start.6 = (s32[1,128]{1,0:T(1,128)S(1)}, s32[1,128]{1,0:T(1,128)S(1)}, u32[]{:S(2)}, u32[]{:S(2)}) collective-permute-start(s32[1,128]{1,0:T(1,128)S(1)} %collective-permute-done.5), channel_id=1, source_target_pairs={{0,1},{1,2},{2,3},{3,4},{4,5},{5,6},{6,7},{7,8},{8,9},{9,10},{10,1... | collective-permute-start | bytes 1544 | tf_op jit(solution)/shard_map/ppermute | solution.py:19
  62.8 8.9 %copy-start.8 = (bf16[1,128,16,128]{3,2,1,0:T(8,128)(2,1)S(1)}, bf16[1,128,16,128]{3,2,1,0:T(8,128)(2,1)}, u32[]{:S(2)}) copy-start(bf16[1,128,16,128]{3,2,1,0:T(8,128)(2,1)} %param.16) | copy-start | bytes 1572868
  63.1 9.6 %collective-permute-start.13 = (s32[1,128]{1,0:T(1,128)S(1)}, s32[1,128]{1,0:T(1,128)S(1)}, u32[]{:S(2)}, u32[]{:S(2)}) collective-permute-start(s32[1,128]{1,0:T(1,128)S(1)} %collective-permute-done.12), channel_id=1, source_target_pairs={{0,15},{1,0},{2,1},{3,2},{4,3},{5,4},{6,5},{7,6},{8,7},{9,8},{10,9... | collective-permute-start | bytes 1544 | tf_op jit(solution)/shard_map/ppermute | solution.py:21
  69.8 9.6 %collective-permute-start.7 = (s32[1,128]{1,0:T(1,128)S(1)}, s32[1,128]{1,0:T(1,128)S(1)}, u32[]{:S(2)}, u32[]{:S(2)}) collective-permute-start(s32[1,128]{1,0:T(1,128)S(1)} %collective-permute-done.6), channel_id=1, source_target_pairs={{0,1},{1,2},{2,3},{3,4},{4,5},{5,6},{6,7},{7,8},{8,9},{9,10},{10,1... | collective-permute-start | bytes 1544 | tf_op jit(solution)/shard_map/ppermute | solution.py:19
  72.7 7.5 %collective-permute-start.14 = (s32[1,128]{1,0:T(1,128)S(1)}, s32[1,128]{1,0:T(1,128)S(1)}, u32[]{:S(2)}, u32[]{:S(2)}) collective-permute-start(s32[1,128]{1,0:T(1,128)S(1)} %collective-permute-done.13), channel_id=1, source_target_pairs={{0,15},{1,0},{2,1},{3,2},{4,3},{5,4},{6,5},{7,6},{8,7},{9,8},{10,9... | collective-permute-start | bytes 1544 | tf_op jit(solution)/shard_map/ppermute | solution.py:21
  79.5 0.7 copy-start.13
  81.8 15.2 %all-to-all-start.1 = ((bf16[128,16,128]{0,2,1:T(8,128)(2,1)}), bf16[128,16,128]{0,2,1:T(8,128)(2,1)S(1)}, u32[]{:S(2)}, u32[]{:S(2)}) async-start(bf16[128,16,128]{0,2,1:T(8,128)(2,1)} %bitcast.12), calls=%async_computation.1 | async-start | bytes 1048576 | tf_op jit(solution)/shard_map/all_to_all | solution.py:173
  88.5 0.7 copy-start.12
  89.2 1.0 copy-start
  97.0 4.7 %copy-start.2 = (bf16[128,16,128]{0,2,1:T(8,128)(2,1)}, bf16[128,16,128]{0,2,1:T(8,128)(2,1)S(1)}, u32[]{:S(2)}) copy-start(bf16[128,16,128]{0,2,1:T(8,128)(2,1)S(1)} %all-to-all-done.1) | copy-start | bytes 1572868
  98.0 15.9 %all-to-all-start.2 = ((bf16[128,16,128]{2,0,1:T(8,128)(2,1)}), bf16[128,16,128]{2,0,1:T(8,128)(2,1)S(1)}, u32[]{:S(2)}, u32[]{:S(2)}) async-start(bf16[128,16,128]{2,0,1:T(8,128)(2,1)} %bitcast.20), calls=%async_computation.2 | async-start | bytes 1048576 | tf_op jit(solution)/shard_map/all_to_all | solution.py:174
  101.7 0.7 copy-start.11
  103.5 14.6 %copy-start.4 = (f32[2048,1,128]{0,2,1:T(8,128)S(1)}, f32[2048,1,128]{0,2,1:T(8,128)}, u32[]{:S(2)}) copy-start(f32[2048,1,128]{0,2,1:T(8,128)} %fusion.33) | copy-start | bytes 3145732
  113.9 14.8 %all-to-all-start.3 = ((bf16[128,16,128]{2,0,1:T(8,128)(2,1)}), bf16[128,16,128]{2,0,1:T(8,128)(2,1)}, u32[]{:S(2)}, u32[]{:S(2)}) async-start(bf16[128,16,128]{2,0,1:T(8,128)(2,1)} %bitcast.129), calls=%async_computation.3 | async-start | bytes 1048576 | tf_op jit(solution)/shard_map/all_to_all | solution.py:172
  121.2 1.0 copy-start.7
  130.0 0.8 copy-start.5
  137.8 1.1 copy-start.6
  138.9 0.8 copy-start.5
  152.2 1.1 copy-start.6
  153.4 0.8 copy-start.5
  172.3 1.1 copy-start.6
  173.4 0.8 copy-start.5
  197.9 1.1 copy-start.6
  200.4 4.1 %copy-start.3 = (bf16[128,16,128]{0,2,1:T(8,128)(2,1)S(1)}, bf16[128,16,128]{0,2,1:T(8,128)(2,1)}, u32[]{:S(2)}) copy-start(bf16[128,16,128]{0,2,1:T(8,128)(2,1)} %copy-done.2) | copy-start | bytes 1572868
  204.4 1.2 copy-start.1
  209.2 12.5 %all-to-all-start.4 = ((bf16[16,2,8192]{2,1,0:T(2,128)(2,1)}), bf16[16,2,8192]{2,1,0:T(2,128)(2,1)S(1)}, u32[]{:S(2)}, u32[]{:S(2)}) async-start(bf16[16,2,8192]{2,1,0:T(2,128)(2,1)} %reshape.576), calls=%async_computation.4 | async-start | bytes 1048576 | tf_op jit(solution)/shard_map/all_to_all | solution.py:191
  221.8 12.7 %all-to-all-start.5 = ((bf16[16,2,8192]{2,1,0:T(2,128)(2,1)}), bf16[16,2,8192]{2,1,0:T(2,128)(2,1)S(1)}, u32[]{:S(2)}, u32[]{:S(2)}) async-start(bf16[16,2,8192]{2,1,0:T(2,128)(2,1)} %reshape.578), calls=%async_computation.5 | async-start | bytes 1048576 | tf_op jit(solution)/shard_map/all_to_all | solution.py:194
  234.4 127.6 %all-to-all-start.6 = ((bf16[16,2,8192]{2,1,0:T(2,128)(2,1)}), bf16[16,2,8192]{2,1,0:T(2,128)(2,1)S(1)}, u32[]{:S(2)}, u32[]{:S(2)}) async-start(bf16[16,2,8192]{2,1,0:T(2,128)(2,1)} %reshape.580), calls=%async_computation.6 | async-start | bytes 1048576 | tf_op jit(solution)/shard_map/all_to_all | solution.py:197
